TPU v7x, 256 devices: a whole 4x4x8 slice. The times are simulated.
256 devices in a mesh: dp: 32 (over y, x, core), tensor: 8 (over z).
Axes of the slice: x: 4, y: 4, z: 8, core: 2. Of those that a mesh axis runs over, the one named last changes fastest.
Arguments:
- rank_query: bfloat16 [256, 32, 5120], P('dp', None, 'tensor'), may hold values from -4.5 to 4.5
- rank_key: bfloat16 [256, 32, 5120], P('dp', None, 'tensor'), may hold values from -4.5 to 4.5
- rank_value: bfloat16 [256, 32, 5120], P('dp', None, 'tensor'), may hold values from -6 to 6
- rank_resid: bfloat16 [256, 32, 5120], P(('dp', 'tensor')), may hold values from -4 to 4
- out_weight: bfloat16 [5120, 5120], P('tensor', 'dp'), may hold values from -0.25 to 0.25
- rank_gain: bfloat16 [5120], replicated, may hold values from 0.099609375 to 1.8984375
- score_weight: bfloat16 [5120], replicated, may hold values from -0.078125 to 0.078125
- pair_index: int32 [256, 3], P(('dp', 'tensor')), may hold values from 0 to 31, as said below
- cand_rank: int32 [1024, 8], P('dp'), may hold values from 0 to 7, each once within a row
- cand_len: int32 [1024, 8], P('dp'), may hold values from 1 to 8, 39 in all within a row
- blend_owner: int32 [32, 32], P('dp'), may hold values from 0 to 31, each once within a row
- blend_rows: bfloat16 [1024, 8, 8, 4096], P('dp', None, None, 'tensor'), may hold values from -6 to 6
- blend_gain: bfloat16 [4096], replicated, may hold values from 0.099609375 to 1.8984375
- blend_weight: bfloat16 [4096, 3, 2048], P('dp', None, 'tensor'), may hold values from -0.09375 to 0.09375
Outputs:
- rank_hidden: bfloat16 [256, 32, 5120], P(('dp', 'tensor'))
- cand_score: float32 [1024, 8], P('dp')
- blended_qkv: bfloat16 [1024, 24, 3, 2048], P('dp', None, None, 'tensor')
Inputs may be any that keep to these rules, and one draw needn't show every extreme that they name: `pair_index`: column 0 is a prompt of the pair's own group of 32 prompts (pair p belongs to group p // 8); columns 1 and 2 are two different candidates of that prompt. `cand_rank`: each row gives every rank once. `blend_owner`: each row names every group once.
All inputs are finite; a program needn't handle non-finite values.
Results may differ from a plain program's by a relative error of at most 0.024.
Values may be sent and summed in bfloat16 or wider, within the bound.
No kernel may reach another device: no remote copies, remote signals or barrier semaphores. Data moves between devices by JAX's collectives and lax.ppermute only.
A program may use at most 128 MiB of HBM per device.

v0:
```python
import math
import jax
import jax.numpy as jnp
from jax import lax
from jax.sharding import PartitionSpec as P

HR = 40
HDR = 128


def pair_attention(queries, keys_in, values_in, head_count):
    pair_count, length, row_width = queries.shape
    head_size = row_width // head_count
    query_heads = queries.reshape(pair_count, length, head_count, head_size)
    key_heads = keys_in.reshape(pair_count, length, head_count, head_size)
    value_heads = values_in.reshape(pair_count, length, head_count, head_size)
    scores = jnp.einsum(
        "pihd,pjhd->phij", query_heads, key_heads, preferred_element_type=jnp.float32
    ) * (1.0 / math.sqrt(HDR))
    highest = jnp.max(scores, axis=-1, keepdims=True)
    weights = jnp.exp(scores - highest)
    soft_weights = (weights / jnp.sum(weights, axis=-1, keepdims=True)).astype(jnp.bfloat16)
    context = jnp.einsum(
        "phij,pjhd->pihd", soft_weights, value_heads, preferred_element_type=jnp.float32
    )
    return context.astype(jnp.bfloat16).reshape(pair_count * length, row_width)


def encode(rows_in, blend_gain, blend_weight):
    whole_rows = lax.all_gather(rows_in, "tensor", axis=3, tiled=True)
    prompts, pick_count, length, features = whole_rows.shape
    flat_rows = whole_rows.reshape(prompts * pick_count * length, features)
    as_float = flat_rows.astype(jnp.float32)
    scale_rows = lax.rsqrt(jnp.mean(as_float * as_float, axis=-1, keepdims=True) + 1e-06)
    blend_normed = (as_float * scale_rows * blend_gain.astype(jnp.float32)).astype(jnp.bfloat16)
    columns = blend_weight.shape[1] * blend_weight.shape[2]
    portion = lax.all_gather(blend_weight, "dp", axis=0, tiled=True)
    projected = jnp.dot(
        blend_normed, portion.reshape(portion.shape[0], columns), preferred_element_type=jnp.float32
    )
    return projected.astype(jnp.bfloat16).reshape(
        prompts, pick_count * length, blend_weight.shape[1], blend_weight.shape[2]
    )


def body(
    rank_query,
    rank_key,
    rank_value,
    rank_resid,
    out_weight,
    rank_gain,
    score_weight,
    pair_index,
    cand_rank,
    cand_len,
    blend_owner,
    blend_rows,
    blend_gain,
    blend_weight,
):
    tensor_count = lax.axis_size("tensor")
    local_heads = HR // tensor_count
    length = rank_query.shape[1]
    context = pair_attention(rank_query, rank_key, rank_value, local_heads)
    own_pairs = rank_resid.shape[0]
    own_rows = own_pairs * length
    term_rows = jnp.dot(
        context,
        lax.all_gather(out_weight, "dp", axis=1, tiled=True),
        preferred_element_type=jnp.float32,
    )
    summed = lax.psum(term_rows.astype(jnp.bfloat16), "tensor").astype(jnp.float32)
    part_sum = lax.dynamic_slice_in_dim(summed, lax.axis_index("tensor") * own_rows, own_rows, 0)
    mixed_rows = rank_resid.reshape(own_rows, -1).astype(jnp.float32) + part_sum
    mean_square = jnp.mean(mixed_rows * mixed_rows, axis=-1, keepdims=True)
    normed = mixed_rows * lax.rsqrt(mean_square + 1e-05) * rank_gain.astype(jnp.float32)
    rank_hidden = normed.astype(jnp.bfloat16).reshape(rank_resid.shape)
    leading = normed.reshape(own_pairs, length, -1)[:, 0, :]
    pair_logit = jnp.sum(leading * score_weight.astype(jnp.float32), axis=-1)
    prompt_count = cand_rank.shape[0]
    cand_count = cand_rank.shape[1]
    slot_ids = jnp.arange(prompt_count * cand_count, dtype=jnp.int32)
    base_slot = pair_index[:, 0] * cand_count
    upward = jnp.where(
        (base_slot + pair_index[:, 1])[:, None] == slot_ids[None, :], pair_logit[:, None], 0.0
    )
    downward = jnp.where(
        (base_slot + pair_index[:, 2])[:, None] == slot_ids[None, :], pair_logit[:, None], 0.0
    )
    vote_sums = jnp.sum(upward - downward, axis=0).reshape(prompt_count, cand_count)
    cand_score = lax.psum(vote_sums, "tensor")
    places = jnp.arange(3, dtype=jnp.int32)
    matched = cand_rank[:, None, :] == places[None, :, None]
    labels = jnp.arange(cand_count, dtype=jnp.int32)
    chosen = jnp.sum(jnp.where(matched, labels[None, None, :], 0), axis=-1)
    chosen_len = jnp.sum(jnp.where(matched, cand_len[:, None, :], 0), axis=-1)
    prompt_ids = jnp.arange(prompt_count, dtype=jnp.int32)
    picked = blend_rows[prompt_ids[:, None], chosen]
    positions = jnp.arange(blend_rows.shape[2], dtype=jnp.int32)
    live_rows = positions[None, None, :] < chosen_len[:, :, None]
    picked = jnp.where(live_rows[..., None], picked, jnp.zeros((), jnp.bfloat16))
    owners = blend_owner[0]
    sender = jnp.sum(
        jnp.where(owners[None, :] == prompt_ids[:, None], prompt_ids[None, :], 0), axis=1
    )
    outgoing = picked[sender]
    arrived = lax.all_to_all(outgoing, "dp", split_axis=0, concat_axis=0, tiled=True)
    blended_qkv = encode(arrived, blend_gain, blend_weight)
    return (rank_hidden, cand_score, blended_qkv)


def solution(mesh):
    placed = (
        P("dp", None, "tensor"),
        P("dp", None, "tensor"),
        P("dp", None, "tensor"),
        P(("dp", "tensor"), None, None),
        P("tensor", "dp"),
        P(),
        P(),
        P(("dp", "tensor"), None),
        P("dp", None),
        P("dp", None),
        P("dp", None),
        P("dp", None, None, "tensor"),
        P(),
        P("dp", None, "tensor"),
    )
    return jax.shard_map(
        body,
        mesh=mesh,
        in_specs=placed,
        out_specs=(P(("dp", "tensor"), None, None), P("dp", None), P("dp", None, None, "tensor")),
        check_vma=False,
    )
```

profile of v0, /device:TPU:2, one launch (start us, length us, event | category | flops | bytes accessed | tf_op | source)
XLA Modules:
  0.0 343.9 jit_solution(1360914309973684097)
XLA Ops:
  7.2 0.0 copy-start
  7.2 0.0 copy-start.3
  7.2 0.0 copy-start.2
  7.2 0.0 all-gather.6.cloned.1.call-start
  7.2 0.9 select_reduce_fusion.2
  8.1 0.1 copy.60
  8.2 0.1 reshape.142
  8.3 0.1 copy.59
  8.4 0.1 iota_compare_fusion
  8.5 0.8 select_reduce_fusion
  9.3 0.6 pad_clamp_fusion
  9.9 2.0 gather_fusion
  11.9 1.3 broadcast_select_fusion
  13.3 0.0 copy-start.5
  13.3 0.0 copy-start.6
  13.3 1.7 gather_fusion.1
  15.0 21.0 %all_to_all.5 = bf16[32,3,8,512]{3,2,1,0:T(8,128)(2,1)} all-to-all(bf16[32,3,8,512]{3,2,1,0:T(8,128)(2,1)} %gather_fusion.1), channel_id=1, replica_groups=mesh['dp'=32,'tensor'=8] {'dp'}, dimensions={0} | all-to-all | bytes 1572864 | tf_op jit(solution)/shard_map/all_to_all | solution.py:108
  36.0 0.0 all-gather.6.cloned.1.call-update
  36.1 0.0 all-gather.4.cloned.1.call-start
  36.1 0.7 all-gather.4.cloned.1.call-update
  36.8 0.0 all-gather.8.cloned.1.call-start
  36.9 1.7 copy.63
  38.6 0.0 all-gather.8.cloned.1.call-update
  38.6 0.0 all-reduce.2.cloned.1.call-start
  38.7 1.0 fusion.32
  39.7 0.3 convolution_multiply_fusion
  40.0 1.3 fusion.6
  41.3 0.2 copy.58
  41.5 0.6 fusion.31
  44.0 0.7 convert_element_type.58
  44.7 66.2 %all-gather.6.cloned.1.call-done = bf16[32,3,8,4096]{3,2,1,0:T(8,128)(2,1)} async-done(((bf16[32,3,8,512]{3,2,1,0:T(8,128)(2,1)}), bf16[32,3,8,4096]{3,2,1,0:T(8,128)(2,1)}) %all-gather.6.cloned.1.call-update) | async-done | bytes 6291472 | tf_op jit(solution)/shard_map/all_gather | solution.py:30
  110.9 4.1 %fusion.1 = f32[32,3,8]{2,1,0:T(4,128)S(1)} fusion(bf16[32,3,8,4096]{3,2,1,0:T(8,128)(2,1)} %all-gather.6.cloned.1.call-done), kind=kLoop, calls=%fused_computation.5 | loop fusion | flops 9436416 | bytes 6294528 | tf_op jit(solution)/shard_map/reduce_sum | solution.py:34
  115.0 0.1 copy.61
  115.1 0.1 copy.62
  115.2 50.6 %all-gather.4.cloned.1.call-done = bf16[640,5120]{0,1:T(8,128)(2,1)} async-done(((bf16[640,160]{0,1:T(8,128)(2,1)}), bf16[640,5120]{0,1:T(8,128)(2,1)}) %all-gather.4.cloned.1.call-update) | async-done | bytes 6553616 | tf_op jit(solution)/shard_map/all_gather | solution.py:70
  165.7 6.6 %convolution_convert_fusion = bf16[256,5120]{1,0:T(8,128)(2,1)} fusion(bf16[640,5120]{0,1:T(8,128)(2,1)} %all-gather.4.cloned.1.call-done, bf16[32,8,5,128]{3,2,1,0:T(8,128)(2,1)S(1)} %bitcast.74), kind=kOutput, calls=%fused_computation.8 | convolution fusion | flops 1679032320 | bytes 9502720 | tf_op jit(solution)/shard_map/dot_general | solution.py:68
  172.3 0.0 all-reduce.2.cloned.1.call-update
  172.4 8.2 %fusion.3 = bf16[32,3,8,4096]{3,2,1,0:T(8,128)(2,1)} fusion(bf16[32,3,8,4096]{3,2,1,0:T(8,128)(2,1)} %all-gather.6.cloned.1.call-done, f32[4096]{0:T(1024)S(1)} %convert_element_type.58, f32[32,3,8]{2,1,0:T(4,128)S(1)} %copy.62), kind=kLoop, calls=%fused_computation.7 | loop fusion | flops 12582912 | bytes 12602368 | tf_op jit(solution)/shard_map/convert_element_type | solution.py:35
  180.5 47.1 %all-gather.8.cloned.1.call-done = bf16[4096,3,256]{0,2,1:T(8,128)(2,1)} async-done(((bf16[128,3,256]{0,2,1:T(8,128)(2,1)}), bf16[4096,3,256]{0,2,1:T(8,128)(2,1)}) %all-gather.8.cloned.1.call-update) | async-done | bytes 6291472 | tf_op jit(solution)/shard_map/all_gather | solution.py:37
  227.7 9.9 %convolution_convert_fusion.1 = bf16[768,768]{1,0:T(8,128)(2,1)} fusion(bf16[768,4096]{1,0:T(8,128)(2,1)} %bitcast.72, bf16[4096,768]{0,1:T(8,128)(2,1)} %bitcast.76), kind=kOutput, calls=%fused_computation.9 | convolution fusion | flops 4832428032 | bytes 13762560 | tf_op jit(solution)/shard_map/dot_general | solution.py:38
  237.6 3.7 %reshape.140 = bf16[32,24,3,256]{3,2,1,0:T(4,128)(2,1)} reshape(bf16[768,768]{1,0:T(8,128)(2,1)} %convolution_convert_fusion.1) | data formatting | bytes 2359296 | tf_op jit(solution)/shard_map/reshape | solution.py:41
  241.3 2.6 copy.64
  243.9 72.1 %all-reduce.2.cloned.1.call-done = bf16[256,5120]{1,0:T(8,128)(2,1)} async-done(((bf16[256,5120]{1,0:T(8,128)(2,1)}), bf16[256,5120]{1,0:T(8,128)(2,1)}) %all-reduce.2.cloned.1.call-update) | async-done | bytes 2621456 | tf_op jit(solution)/shard_map/psum | solution.py:73
  316.0 1.2 multiply_reduce_fusion
  317.2 1.8 fusion.7
  319.1 0.6 multiply_reduce_fusion.1
  319.7 0.6 select_subtract_fusion
  320.2 17.1 %psum.15 = f32[32,8]{0,1:T(8,128)} all-reduce(f32[32,8]{0,1:T(8,128)S(1)} %select_subtract_fusion), channel_id=1, replica_groups=mesh['dp'=32,'tensor'=8] {'tensor'}, use_global_device_ids=true, to_apply=%region_5.6 | all-reduce | flops 256 | bytes 2048 | tf_op jit(solution)/shard_map/psum | solution.py:92
  (15 shorter events, 0.1 us)
Async XLA Ops:
  7.2 2.7 copy-start
  7.2 31.5 %copy-start.3 = (bf16[8,32,640]{2,1,0:T(8,128)(2,1)S(1)}, bf16[8,32,640]{2,1,0:T(8,128)(2,1)}, u32[]{:S(2)}) copy-start(bf16[8,32,640]{2,1,0:T(8,128)(2,1)} %param.14) | copy-start | bytes 983044
  7.2 31.5 %copy-start.2 = (bf16[8,32,640]{2,1,0:T(8,128)(2,1)S(1)}, bf16[8,32,640]{2,1,0:T(8,128)(2,1)}, u32[]{:S(2)}) copy-start(bf16[8,32,640]{2,1,0:T(8,128)(2,1)} %param.15) | copy-start | bytes 983044
  7.2 103.7 %all-gather.6.cloned.1.call-start = ((), (), s32[]{:S(2)}) async-start(), calls=%async_computation.3 | async-start | bytes 7077888 | tf_op jit(solution)/shard_map/all_gather | solution.py:30
  13.3 28.3 %copy-start.5 = (bf16[5120]{0:T(1024)(128)(2,1)S(1)}, bf16[5120]{0:T(1024)(128)(2,1)}, u32[]{:S(2)}) copy-start(bf16[5120]{0:T(1024)(128)(2,1)} %param.19) | copy-start | bytes 30724
  13.3 28.3 %copy-start.6 = (s32[1,3]{1,0:T(1,128)S(1)}, s32[1,3]{1,0:T(1,128)}, u32[]{:S(2)}) copy-start(s32[1,3]{1,0:T(1,128)} %param.21) | copy-start | bytes 40
  36.1 129.7 %all-gather.4.cloned.1.call-start = ((), (), s32[]{:S(2)}) async-start(), calls=%async_computation.1 | async-start | bytes 6758400 | tf_op jit(solution)/shard_map/all_gather | solution.py:70
  36.8 190.9 %all-gather.8.cloned.1.call-start = ((), (), s32[]{:S(2)}) async-start(), calls=%async_computation.4 | async-start | bytes 6488064 | tf_op jit(solution)/shard_map/all_gather | solution.py:37
  38.6 277.4 %all-reduce.2.cloned.1.call-start = ((), (), s32[]{:S(2)}) async-start(), calls=%async_computation.2 | async-start | bytes 5242880 | tf_op jit(solution)/shard_map/psum | solution.py:73
  227.7 88.3 %copy-start.1 = (bf16[1,32,5120]{2,1,0:T(8,128)(2,1)S(1)}, bf16[1,32,5120]{2,1,0:T(8,128)(2,1)}, u32[]{:S(2)}) copy-start(bf16[1,32,5120]{2,1,0:T(8,128)(2,1)} %param.17) | copy-start | bytes 983044
  237.6 81.5 %copy-start.4 = (bf16[5120]{0:T(1024)(128)(2,1)S(1)}, bf16[5120]{0:T(1024)(128)(2,1)}, u32[]{:S(2)}) copy-start(bf16[5120]{0:T(1024)(128)(2,1)} %param.20) | copy-start | bytes 30724
Sparse Core Ops, SparseCore 0:
  36.2 74.6 all-gather.5
  113.4 52.2 all-gather.3
  168.8 58.8 all-gather.7
  229.9 86.0 all-reduce.1
where the time goes:
time: 345 us; the launch traced here: 344 us
  waiting for transfers between devices  237 us (69%)
  blocking collectives  38.1 us (11%)
  other arithmetic  20.9 us (6%)
  matrix products  19.1 us (6%)
  between operations  15.8 us (5%)
  local copies, waits for them, and re-layouts  13.1 us (4%)
    psum x1, waiting for transfers between devices, body(): lax.psum(term_rows.astype(jnp.bfloat16), 'tensor').astype(jnp.float32)  72.1 us
    all_gather x1, waiting for transfers between devices, encode(): whole_rows = lax.all_gather(rows_in, 'tensor', axis=3, tiled=True)  66.2 us
    all_gather x1, waiting for transfers between devices, body(): lax.all_gather(out_weight, 'dp', axis=1, tiled=True)  50.6 us
    all_gather x1, waiting for transfers between devices, encode(): portion = lax.all_gather(blend_weight, 'dp', axis=0, tiled=True)  47.1 us
    all_to_all x1, blocking collectives, body(): lax.all_to_all(outgoing, 'dp', split_axis=0, concat_axis=0, tiled=True)  21 us
    psum x1, blocking collectives, body(): cand_score = lax.psum(vote_sums, 'tensor')  17.1 us
    dot_general x1, matrix products, encode(): jnp.dot(blend_normed, portion.reshape(portion.shape[0], columns), preferr...  9.89 us
    convert_element_type x1, other arithmetic, encode(): (as_float * scale_rows * blend_gain.astype(jnp.float32)).astype(jnp.bfloa...  8.16 us
  transfers between devices with their start and end apart: 4, of which 4 were waited for; matrix products, arithmetic and copies ran while one was open for 12% of the time, Pallas kernels for 0%

commit v1 on v0

--- a/solution.py
+++ b/solution.py
@@ -34,7 +34,9 @@
     scale_rows = lax.rsqrt(jnp.mean(as_float * as_float, axis=-1, keepdims=True) + 1e-06)
     blend_normed = (as_float * scale_rows * blend_gain.astype(jnp.float32)).astype(jnp.bfloat16)
     columns = blend_weight.shape[1] * blend_weight.shape[2]
-    portion = lax.all_gather(blend_weight, "dp", axis=0, tiled=True)
+    portion = jnp.concatenate(
+        lax.all_to_all(jnp.stack([blend_weight] * lax.axis_size("dp")), "dp", 0, 0), axis=0
+    )
     projected = jnp.dot(
         blend_normed, portion.reshape(portion.shape[0], columns), preferred_element_type=jnp.float32
     )

time: 345 us -> 286 us (0.83)
  waiting for transfers between devices: 237 us -> 165 us
  local copies, waits for them, and re-layouts: 13.1 us -> 25 us
  starting transfers between devices: 0.16 us -> 6.42 us
  other arithmetic: 20.9 us -> 16.9 us
    all_to_all x0 -> x1, waiting for transfers between devices: none -> 70.3 us  [encode(): lax.all_to_all(jnp.stack([blend_weight] * lax.axis_size('dp')), 'dp', 0, 0)]
    all_gather x1, waiting for transfers between devices: 66.2 us -> 0.01 us  [encode(): whole_rows = lax.all_gather(rows_in, 'tensor', axis=3, tiled=True)]
    all_gather x1 -> x0, waiting for transfers between devices: 47.1 us -> none  [encode(): portion = lax.all_gather(blend_weight, 'dp', axis=0, tiled=True)]
    all_gather x1, waiting for transfers between devices: 50.6 us -> 29.3 us  [body(): lax.all_gather(out_weight, 'dp', axis=1, tiled=True)]
    all_to_all x0 -> x1, local copies, waits for them, and re-layouts: none -> 9.57 us  [encode(): lax.all_to_all(jnp.stack([blend_weight] * lax.axis_size('dp')), 'dp', 0, 0)]
    psum x1, waiting for transfers between devices: 72.1 us -> 64.8 us  [body(): lax.psum(term_rows.astype(jnp.bfloat16), 'tensor').astype(jnp.float32)]
    all_to_all x0 -> x1, starting transfers between devices: none -> 6.12 us  [encode(): lax.all_to_all(jnp.stack([blend_weight] * lax.axis_size('dp')), 'dp', 0, 0)]
    another operation x0 -> x1, local copies, waits for them, and re-layouts: none -> 4.15 us  [encode(): jnp.stack([blend_weight] * lax.axis_size('dp'))]
  transfers between devices with their start and end apart: 4 -> 4, of which waited for: 4 -> 3; matrix products, arithmetic and copies ran while one was open for 12% -> 15% of each run, Pallas kernels for 0% -> 0%
where the time goes in v1:
time: 286 us; the launch traced here: 285 us
  waiting for transfers between devices  165 us (58%)
  blocking collectives  38.1 us (13%)
  local copies, waits for them, and re-layouts  25 us (9%)
  matrix products  18 us (6%)
  other arithmetic  16.9 us (6%)
  between operations  15.9 us (6%)
  starting transfers between devices  6.42 us (2%)
    all_to_all x1, waiting for transfers between devices, encode(): lax.all_to_all(jnp.stack([blend_weight] * lax.axis_size('dp')), 'dp', 0, 0)  70.3 us
    psum x1, waiting for transfers between devices, body(): lax.psum(term_rows.astype(jnp.bfloat16), 'tensor').astype(jnp.float32)  64.8 us
    all_gather x1, waiting for transfers between devices, body(): lax.all_gather(out_weight, 'dp', axis=1, tiled=True)  29.3 us
    all_to_all x1, blocking collectives, body(): lax.all_to_all(outgoing, 'dp', split_axis=0, concat_axis=0, tiled=True)  21 us
    psum x1, blocking collectives, body(): cand_score = lax.psum(vote_sums, 'tensor')  17.1 us
    all_to_all x1, local copies, waits for them, and re-layouts, encode(): lax.all_to_all(jnp.stack([blend_weight] * lax.axis_size('dp')), 'dp', 0, 0)  9.57 us
    dot_general x1, matrix products, encode(): jnp.dot(blend_normed, portion.reshape(portion.shape[0], columns), preferr...  9.4 us
    dot_general x1, matrix products, body(): jnp.dot(context, lax.all_gather(out_weight, 'dp', axis=1, tiled=True), pr...  6.59 us
  transfers between devices with their start and end apart: 4, of which 3 were waited for; matrix products, arithmetic and copies ran while one was open for 15% of the time, Pallas kernels for 0%

profile of v1, /device:TPU:2, one launch (start us, length us, event | category | flops | bytes accessed | tf_op | source)
XLA Modules:
  0.0 285.4 jit_solution(15469259685644402701)
XLA Ops:
  7.2 0.0 copy-start
  7.2 0.0 copy-start.4
  7.2 0.0 all-gather.5.cloned.1.call-start
  7.2 0.9 select_reduce_fusion
  8.2 0.7 select_reduce_fusion.2
  8.9 0.1 copy.74
  9.0 0.1 reshape.140
  9.1 0.1 copy.73
  9.2 0.1 iota_compare_fusion
  9.3 0.0 copy-done
  9.3 2.0 gather_fusion
  11.4 1.3 broadcast_select_fusion
  12.7 1.5 gather_fusion.1
  14.1 21.0 %all_to_all.10 = bf16[32,3,8,512]{3,2,1,0:T(8,128)(2,1)} all-to-all(bf16[32,3,8,512]{3,2,1,0:T(8,128)(2,1)} %gather_fusion.1), channel_id=1, replica_groups=mesh['dp'=32,'tensor'=8] {'dp'}, dimensions={0} | all-to-all | bytes 1572864 | tf_op jit(solution)/shard_map/all_to_all | solution.py:110
  35.2 0.0 all-gather.5.cloned.1.call-update
  35.2 0.0 all-gather.3.cloned.1.call-start
  35.2 0.7 all-gather.3.cloned.1.call-update
  35.9 0.0 copy-done.4
  36.0 0.2 copy.77
  36.1 4.1 %stack.2 = bf16[32,128,3,256]{1,3,2,0:T(8,128)(2,1)} broadcast(bf16[128,3,256]{0,2,1:T(8,128)(2,1)S(1)} %copy.77), dimensions={1,2,3} | broadcast | bytes 6488064 | tf_op jit(solution)/shard_map/stack | solution.py:38
  40.3 0.0 copy-start.3
  40.3 6.1 %all-to-all-start.1 = ((bf16[32,128,3,256]{1,3,2,0:T(8,128)(2,1)}), bf16[32,128,3,256]{1,3,2,0:T(8,128)(2,1)}, u32[]{:S(2)}, u32[]{:S(2)}) async-start(bf16[32,128,3,256]{1,3,2,0:T(8,128)(2,1)} %stack.2), calls=%async_computation.1 | async-start | bytes 12582912 | tf_op jit(solution)/shard_map/all_to_all | solution.py:38
  46.4 0.2 all-reduce.2.cloned.1.call-start
  46.7 0.6 fusion.37
  49.3 0.4 fusion.38
  49.6 0.3 convolution_multiply_fusion
  49.9 1.3 fusion.12
  51.2 0.2 copy.72
  51.4 70.3 %all-to-all-done.1 = bf16[32,128,3,256]{1,3,2,0:T(8,128)(2,1)} async-done(((bf16[32,128,3,256]{1,3,2,0:T(8,128)(2,1)}), bf16[32,128,3,256]{1,3,2,0:T(8,128)(2,1)}, u32[]{:S(2)}, u32[]{:S(2)}) %all-to-all-start.1) | async-done | bytes 6291488 | tf_op jit(solution)/shard_map/all_to_all | solution.py:38
  121.7 9.6 %copy.78 = bf16[32,128,3,256]{1,0,3,2:T(8,128)(2,1)} copy(bf16[32,128,3,256]{1,3,2,0:T(8,128)(2,1)} %all-to-all-done.1) | data formatting | bytes 12582912 | tf_op jit(solution)/shard_map/all_to_all | solution.py:38
  131.3 4.2 %fusion.1 = f32[32,3,8]{2,1,0:T(4,128)S(1)} fusion(bf16[32,3,8,4096]{3,2,1,0:T(8,128)(2,1)} %all-gather.5.cloned.1.call-done), kind=kLoop, calls=%fused_computation.5 | loop fusion | flops 9436416 | bytes 6294528 | tf_op jit(solution)/shard_map/reduce_sum | solution.py:34
  135.4 0.1 copy.75
  135.5 29.3 %all-gather.3.cloned.1.call-done = bf16[640,5120]{0,1:T(8,128)(2,1)} async-done(((bf16[640,160]{0,1:T(8,128)(2,1)}), bf16[640,5120]{0,1:T(8,128)(2,1)}) %all-gather.3.cloned.1.call-update) | async-done | bytes 6553616 | tf_op jit(solution)/shard_map/all_gather | solution.py:72
  164.9 6.6 %convolution_convert_fusion = bf16[256,5120]{1,0:T(8,128)(2,1)} fusion(bf16[640,5120]{0,1:T(8,128)(2,1)} %all-gather.3.cloned.1.call-done, bf16[32,8,5,128]{3,2,1,0:T(8,128)(2,1)S(1)} %bitcast.82), kind=kOutput, calls=%fused_computation.8 | convolution fusion | flops 1679032320 | bytes 9502720 | tf_op jit(solution)/shard_map/dot_general | solution.py:70
  171.5 0.0 all-reduce.2.cloned.1.call-update
  171.5 0.1 copy.76
  171.6 5.3 %fusion.3 = bf16[32,3,8,4096]{3,2,1,0:T(8,128)(2,1)S(1)} fusion(bf16[32,3,8,4096]{3,2,1,0:T(8,128)(2,1)} %all-gather.5.cloned.1.call-done, f32[4096]{0:T(1024)S(1)} %convert_element_type.58, f32[32,3,8]{2,1,0:T(4,128)S(1)} %copy.76), kind=kLoop, calls=%fused_computation.7 | loop fusion | flops 12582912 | bytes 12602368 | tf_op jit(solution)/shard_map/convert_element_type | solution.py:35
  176.9 0.0 copy-start.1
  177.0 9.4 %fusion.7 = bf16[768,768]{1,0:T(8,128)(2,1)} fusion(bf16[768,4096]{1,0:T(8,128)(2,1)S(1)} %bitcast.80, bf16[96,8,32,128]{3,2,1,0:T(8,128)(2,1)} %bitcast.79), kind=kOutput, calls=%fused_computation.12 | convolution fusion | flops 4832428032 | bytes 13762560 | tf_op jit(solution)/shard_map/dot_general | solution.py:40
  186.4 3.7 %reshape.138 = bf16[32,24,3,256]{3,2,1,0:T(4,128)(2,1)} reshape(bf16[768,768]{1,0:T(8,128)(2,1)} %fusion.7) | data formatting | bytes 2359296 | tf_op jit(solution)/shard_map/reshape | solution.py:43
  190.1 2.6 copy.79
  192.7 64.8 %all-reduce.2.cloned.1.call-done = bf16[256,5120]{1,0:T(8,128)(2,1)} async-done(((bf16[256,5120]{1,0:T(8,128)(2,1)}), bf16[256,5120]{1,0:T(8,128)(2,1)}) %all-reduce.2.cloned.1.call-update) | async-done | bytes 2621456 | tf_op jit(solution)/shard_map/psum | solution.py:75
  257.5 1.2 multiply_reduce_fusion
  258.7 1.8 fusion.13
  260.5 0.0 copy-done.5
  260.5 0.6 multiply_reduce_fusion.1
  261.2 0.7 select_subtract_fusion
  261.8 17.1 %psum.15 = f32[32,8]{0,1:T(8,128)} all-reduce(f32[32,8]{0,1:T(8,128)S(1)} %select_subtract_fusion), channel_id=1, replica_groups=mesh['dp'=32,'tensor'=8] {'tensor'}, use_global_device_ids=true, to_apply=%region_5.6 | all-reduce | flops 256 | bytes 2048 | tf_op jit(solution)/shard_map/psum | solution.py:94
  (20 shorter events, 0.1 us)
Async XLA Ops:
  7.2 2.1 copy-start
  7.2 28.8 %copy-start.4 = (bf16[128,3,256]{2,0,1:T(8,128)(2,1)S(1)}, bf16[128,3,256]{2,0,1:T(8,128)(2,1)}, u32[]{:S(2)}) copy-start(bf16[128,3,256]{2,0,1:T(8,128)(2,1)} %param.27) | copy-start | bytes 589828
  7.2 124.1 %all-gather.5.cloned.1.call-start = ((), (), s32[]{:S(2)}) async-start(), calls=%async_computation.4 | async-start | bytes 7077888 | tf_op jit(solution)/shard_map/all_gather | solution.py:30
  35.2 129.7 %all-gather.3.cloned.1.call-start = ((), (), s32[]{:S(2)}) async-start(), calls=%async_computation.2 | async-start | bytes 6758400 | tf_op jit(solution)/shard_map/all_gather | solution.py:72
  40.3 6.4 %copy-start.8 = (s32[1,3]{1,0:T(1,128)S(1)}, s32[1,3]{1,0:T(1,128)}, u32[]{:S(2)}) copy-start(s32[1,3]{1,0:T(1,128)} %param.21) | copy-start | bytes 40
  40.3 8.9 %copy-start.7 = (bf16[4096]{0:T(1024)(128)(2,1)S(1)}, bf16[4096]{0:T(1024)(128)(2,1)}, u32[]{:S(2)}) copy-start(bf16[4096]{0:T(1024)(128)(2,1)} %param.26) | copy-start | bytes 24580
  40.3 8.9 %copy-start.6 = (bf16[5120]{0:T(1024)(128)(2,1)S(1)}, bf16[5120]{0:T(1024)(128)(2,1)}, u32[]{:S(2)}) copy-start(bf16[5120]{0:T(1024)(128)(2,1)} %param.19) | copy-start | bytes 30724
  40.3 9.0 %copy-start.2 = (bf16[8,32,640]{2,1,0:T(8,128)(2,1)S(1)}, bf16[8,32,640]{2,1,0:T(8,128)(2,1)}, u32[]{:S(2)}) copy-start(bf16[8,32,640]{2,1,0:T(8,128)(2,1)} %param.15) | copy-start | bytes 983044
  40.3 9.0 %copy-start.3 = (bf16[8,32,640]{2,1,0:T(8,128)(2,1)S(1)}, bf16[8,32,640]{2,1,0:T(8,128)(2,1)}, u32[]{:S(2)}) copy-start(bf16[8,32,640]{2,1,0:T(8,128)(2,1)} %param.14) | copy-start | bytes 983044
  40.3 81.4 %all-to-all-start.1 = ((bf16[32,128,3,256]{1,3,2,0:T(8,128)(2,1)}), bf16[32,128,3,256]{1,3,2,0:T(8,128)(2,1)}, u32[]{:S(2)}, u32[]{:S(2)}) async-start(bf16[32,128,3,256]{1,3,2,0:T(8,128)(2,1)} %stack.2), calls=%async_computation.1 | async-start | bytes 12582912 | tf_op jit(solution)/shard_map/all_to_all | solution.py:38
  46.4 211.1 %all-reduce.2.cloned.1.call-start = ((), (), s32[]{:S(2)}) async-start(), calls=%async_computation.3 | async-start | bytes 5242880 | tf_op jit(solution)/shard_map/psum | solution.py:75
  176.9 80.5 %copy-start.1 = (bf16[1,32,5120]{2,1,0:T(8,128)(2,1)S(1)}, bf16[1,32,5120]{2,1,0:T(8,128)(2,1)}, u32[]{:S(2)}) copy-start(bf16[1,32,5120]{2,1,0:T(8,128)(2,1)} %param.17) | copy-start | bytes 983044
  186.4 74.2 %copy-start.5 = (bf16[5120]{0:T(1024)(128)(2,1)S(1)}, bf16[5120]{0:T(1024)(128)(2,1)}, u32[]{:S(2)}) copy-start(bf16[5120]{0:T(1024)(128)(2,1)} %param.20) | copy-start | bytes 30724
Sparse Core Ops, SparseCore 0:
  35.3 74.6 all-gather.4
  112.5 52.3 all-gather.2
  171.6 85.8 all-reduce.1
